TPU v7x, 32 devices: a whole 2x2x4 slice. The times are simulated.
32 devices in a mesh: tm: 8 (over z, y), emit: 4 (over x, core).
Axes of the slice: x: 2, y: 2, z: 4, core: 2. Of those that a mesh axis runs over, the one named last changes fastest.
Arguments:
- observed: int32 [8, 512], P('emit', 'tm'), may hold values from 0 to 4095
- starts: int32 [8], P('emit'), may hold values from 0 to 255
- initial: float32 [256], replicated, may hold values from 0.1 to 1
- transition: float32 [256, 256], replicated, may hold values from 0 to 1, as said below
- emission: float32 [4096, 256], P('emit'), may hold values from 0.5 to 2
Outputs:
- posterior: float32 [8, 512, 256], P('emit', 'tm')
- new_emission: float32 [4096, 256], P(('tm', 'emit'))
- loglik: float32 [8], P('emit')
Inputs may be any that keep to these rules, and one draw needn't show every extreme that they name: `transition`: entries positive.
All inputs are finite; a program needn't handle non-finite values.
Results may differ from a plain program's by a relative error of at most 0.0003.
Values sent between devices are 32-bit elements; how exact they have to be, the bound alone decides.
No kernel may reach another device: no remote copies, remote signals or barrier semaphores. Data moves between devices by JAX's collectives and lax.ppermute only.
A program may use at most 128 MiB of HBM per device.

v0:
```python
import jax
import jax.numpy as jnp
from jax import lax
from jax.sharding import PartitionSpec as P

highest = lax.Precision.HIGHEST
pseudo_count = 0.01


def from_behind(value, axis, by):
    peers = lax.axis_size(axis)
    pairs = [(i, i + by) for i in range(peers) if 0 <= i + by < peers]
    return lax.ppermute(value, axis, pairs)


def normalize_rows(values):
    return values / jnp.sum(values, axis=-1, keepdims=True)


def normalize_blocks(matrices):
    return matrices / jnp.sum(matrices, axis=(1, 2), keepdims=True)


def shards(observed, starts, initial, transition, emission):
    traj_rows, frame_count = observed.shape
    states = transition.shape[0]
    tm_count = lax.axis_size("tm")
    tm_place = lax.axis_index("tm")
    emit_count = lax.axis_size("emit")
    own_rows = emission.shape[0]
    total_rows = own_rows * emit_count
    positions = tm_place * frame_count + jnp.arange(frame_count, dtype=jnp.int32)
    active = positions[None, :] >= starts[:, None]
    block_rows = lax.all_gather(emission, "emit", axis=0, tiled=True)
    local_ids = observed
    inside = (local_ids >= 0) & (local_ids < block_rows.shape[0])
    taken = jnp.take(block_rows, jnp.clip(local_ids, 0, block_rows.shape[0] - 1), axis=0)
    weights = jnp.where(inside[:, :, None], taken, 0.0)
    weight_seq = jnp.swapaxes(weights, 0, 1)
    active_seq = active.T
    eye_block = jnp.broadcast_to(jnp.eye(states, dtype=jnp.float32), (traj_rows, states, states))

    def product_step(carried, inputs):
        weight_now, active_now = inputs
        moved = (
            jnp.einsum("nij,jk->nik", carried, transition, precision=highest)
            * weight_now[:, None, :]
        )
        moved = normalize_blocks(moved)
        return (jnp.where(active_now[:, None, None], moved, carried), None)

    transfer, _ = lax.scan(product_step, eye_block, (weight_seq, active_seq))
    prior_state = jnp.broadcast_to(initial / jnp.sum(initial), (traj_rows, states))
    final_state = jnp.full((traj_rows, states), 1.0 / states, jnp.float32)

    def relay_round(round_index, carried):
        forward_in, backward_in = carried
        forward_out = normalize_rows(
            jnp.einsum("ni,nij->nj", forward_in, transfer, precision=highest)
        )
        backward_out = normalize_rows(
            jnp.einsum("nij,nj->ni", transfer, backward_in, precision=highest)
        )
        from_left = from_behind(forward_out, "tm", 1)
        from_right = from_behind(backward_out, "tm", -1)
        forward_in = jnp.where(tm_place == 0, prior_state, from_left)
        backward_in = jnp.where(tm_place == tm_count - 1, final_state, from_right)
        return (forward_in, backward_in)

    forward_in, backward_in = lax.fori_loop(
        0, tm_count - 1, relay_round, (prior_state, final_state)
    )

    def forward_step(previous, inputs):
        weight_now, active_now = inputs
        moved = jnp.dot(previous, transition, precision=highest) * weight_now
        scaling = jnp.sum(moved, axis=1)
        updated = jnp.where(active_now[:, None], moved / scaling[:, None], previous)
        return (updated, (updated, jnp.where(active_now, jnp.log(scaling), 0.0)))

    _, (forward, log_scales) = lax.scan(forward_step, forward_in, (weight_seq, active_seq))

    def backward_step(later_msg, inputs):
        weight_now, active_now = inputs
        moved = jnp.dot(later_msg * weight_now, transition.T, precision=highest)
        earlier = jnp.where(active_now[:, None], normalize_rows(moved), later_msg)
        return (earlier, later_msg)

    _, backward = lax.scan(backward_step, backward_in, (weight_seq, active_seq), reverse=True)
    joint_prob = forward * backward
    occupancy = jnp.where(active_seq[:, :, None], normalize_rows(joint_prob), 0.0)
    posterior = jnp.swapaxes(states * occupancy, 0, 1)
    loglik_local = jnp.sum(log_scales, axis=0)
    occ_rows = jnp.swapaxes(occupancy, 0, 1).reshape(-1, states)
    frame_list = observed.reshape(-1)
    block = total_rows // (tm_count * emit_count)
    local_ids = frame_list
    inside = (local_ids >= 0) & (local_ids < block * lax.axis_size(("tm", "emit")))
    counts = lax.psum_scatter(
        jax.ops.segment_sum(
            jnp.where(inside[:, None], occ_rows, 0.0),
            jnp.clip(local_ids, 0, block * lax.axis_size(("tm", "emit")) - 1),
            num_segments=block * lax.axis_size(("tm", "emit")),
        ),
        ("tm", "emit"),
        scatter_dimension=0,
        tiled=True,
    )
    totals = lax.psum(jnp.sum(counts, axis=0), ("tm", "emit"))
    loglik_sum = lax.psum(loglik_local, "tm")
    new_emission = total_rows * (counts + pseudo_count) / (totals + total_rows * pseudo_count)
    loglik = loglik_sum / (frame_count * tm_count - starts).astype(jnp.float32)
    return (posterior, new_emission, loglik)


def solution(mesh):
    in_specs = (P("emit", "tm"), P("emit"), P(), P(), P("emit", None))
    out_specs = (P("emit", "tm", None), P(("tm", "emit"), None), P("emit"))
    return jax.shard_map(shards, mesh=mesh, in_specs=in_specs, out_specs=out_specs, check_vma=False)
```

profile of v0, /device:TPU:10, one launch (start us, length us, event | category | flops | bytes accessed | tf_op | source)
XLA Modules:
  0.0 506.8 jit_solution(13056474050517089215)
XLA Ops:
  13.1 31.2 %all-gather.2.cloned.1.call-done = f32[4096,256]{1,0:T(8,128)} async-done(((f32[1024,256]{1,0:T(8,128)}), f32[4096,256]{1,0:T(8,128)}) %all-gather.2.cloned.1.call-update) | async-done | bytes 4194320 | tf_op jit(solution)/shard_map/all_gather | solution.py:34
  44.2 2.9 gather_fusion
  47.4 117.4 %while.55 = (s32[]{:T(128)}, f32[2,256,256]{2,1,0:T(8,128)S(1)}, pred[64,2]{1,0:T(8,128)(4,1)S(1)}, f32[256,256]{1,0:T(8,128)}, f32[64,2,256]{2,1,0:T(2,128)S(1)}, /*index=5*/s32[]{:T(128)}) while((s32[]{:T(128)}, f32[2,256,256]{2,1,0:T(8,128)S(1)}, pred[64,2]{1,0:T(8,128)(4,1)S(1)}, f32[256,256]{1,0:T(8,128)}, f32[64,2,256]{2,1,0:T(2,128)S(1)}, ...), condition=%wide.region_3.4_spmd, body=%wide.region_1.3_spmd.sunk | while | flops 403177472 | bytes 2889835 | solution.py:52
  164.9 68.8 %while.58 = (s32[]{:T(128)}, f32[2,256]{1,0:T(2,128)S(1)}, f32[2,256]{1,0:T(2,128)S(1)}, pred[]{:T(512)}, f32[2,256,256]{2,1,0:T(8,128)S(1)}, /*index=5*/pred[]{:T(512)}, f32[256]{0:T(256)S(1)}, s32[]{:T(128)}, s32[]{:T(128)}) while((s32[]{:T(128)}, f32[2,256]{1,0:T(2,128)S(1)}, f32[2,256]{1,0:T(2,128)S(1)}, pred[]{:T(512)}, ...), condition=%wide.region_7.8_spmd.clone, body=%wide.region_4.7_spmd.clone.sunk | while | flops 3149311 | bytes 1098969 | solution.py:70
  165.6 3.4 collective-permute-start.1
  169.6 2.5 collective-permute-start
  172.1 3.9 collective-permute-done
  179.2 3.9 collective-permute-start
  183.1 2.4 collective-permute-done
  188.8 3.9 collective-permute-start
  192.7 2.4 collective-permute-done
  198.4 3.9 collective-permute-start
  202.4 2.4 collective-permute-done
  208.0 3.9 collective-permute-start
  212.0 2.4 collective-permute-done
  217.6 3.9 collective-permute-start
  221.6 2.4 collective-permute-done
  227.3 3.9 collective-permute-start
  233.7 38.5 %while.57 = (s32[]{:T(128)}, f32[2,256]{1,0:T(2,128)S(1)}, f32[64,2,256]{2,0,1:T(8,128)S(1)}, pred[64,2]{1,0:T(8,128)(4,1)S(1)}, f32[64,2,256]{2,1,0:T(2,128)S(1...) while((s32[]{:T(128)}, f32[2,256]{1,0:T(2,128)S(1)}, f32[64,2,256]{2,0,1:T(8,128)S(1)}, ...), condition=%wide.region_13.14_spmd, body=%wide.region_11.13_spmd.sunk | while | flops 1574913 | bytes 282763 | solution.py:89
  272.2 36.6 %while.56 = (s32[]{:T(128)}, f32[2,256]{1,0:T(2,128)S(1)}, f32[64,2,256]{2,0,1:T(8,128)S(1)}, f32[64,2]{1,0:T(8,128)S(1)}, pred[64,2]{1,0:T(8,128)(4,1)S(1)}, /*...) while((s32[]{:T(128)}, f32[2,256]{1,0:T(2,128)S(1)}, ...), condition=%wide.region_10.11_spmd, body=%wide.region_8.10_spmd.sunk | while | flops 1574914 | bytes 282801 | solution.py:81
  309.3 3.4 scatter_custom_fusion
  312.7 20.5 %psum.15 = f32[2]{0:T(128)S(1)} all-reduce(f32[2]{0:T(128)S(1)} %reduce_sum.94), channel_id=1, replica_groups=mesh['tm'=8,'emit'=4] {'tm'}, use_global_device_ids=true, to_apply=%region_20.21 | all-reduce | flops 2 | bytes 16 | tf_op jit(solution)/shard_map/psum | solution.py:110
  334.4 99.9 %reduce-scatter.2.cloned.1.call-done = f32[128,256]{1,0:T(8,128)} async-done(((f32[4096,256]{1,0:T(8,128)}), f32[128,256]{1,0:T(8,128)}) %reduce-scatter.2.cloned.1.call-update) | async-done | bytes 131088 | tf_op jit(solution)/shard_map/reduce_scatter | solution.py:99
  435.3 63.1 %psum.14 = f32[256]{0:T(256)S(1)} all-reduce(f32[256]{0:T(256)S(1)} %reduce_sum.93), channel_id=1, replica_groups=mesh['tm'=8,'emit'=4] {'tm','emit'}, use_global_device_ids=true, to_apply=%region_18.19 | all-reduce | flops 256 | bytes 2048 | tf_op jit(solution)/shard_map/psum | solution.py:109
  (1137 shorter events, 217.7 us)
Async XLA Ops:
  7.2 37.1 %all-gather.2.cloned.1.call-start = ((), (), s32[]{:S(2)}) async-start(), calls=%async_computation.1 | async-start | bytes 5242880 | tf_op jit(solution)/shard_map/all_gather | solution.py:34
  7.9 426.4 %reduce-scatter.2.cloned.1.call-start = ((), (), s32[]{:S(2)}) async-start(), calls=%async_computation.2 | async-start | bytes 4325376 | tf_op jit(solution)/shard_map/reduce_scatter | solution.py:99
  164.8 68.8 %copy-start = (f32[256,256]{1,0:T(8,128)S(1)}, f32[256,256]{1,0:T(8,128)}, u32[]{:S(2)}) copy-start(f32[256,256]{1,0:T(8,128)} %get-tuple-element.664) | copy-start | bytes 786436
  165.6 6.4 %collective-permute-start.1 = (f32[2,256]{1,0:T(2,128)S(1)}, f32[2,256]{1,0:T(2,128)S(1)}, u32[]{:S(2)}, u32[]{:S(2)}) collective-permute-start(f32[2,256]{1,0:T(2,128)S(1)} %bitcast_divide_fusion.5), channel_id=1, source_target_pairs={{4,0},{8,4},{12,8},{16,12},{20,16},{24,20},{28,24},{5,1},{9,5},{13... | collective-permute-start | bytes 6152 | tf_op jit(solution)/shard_map/while/body/eval_jaxpr/ppermute | solution.py:13
  169.6 6.4 %collective-permute-start = (f32[2,256]{1,0:T(2,128)S(1)}, f32[2,256]{1,0:T(2,128)S(1)}, u32[]{:S(2)}, u32[]{:S(2)}) collective-permute-start(f32[2,256]{1,0:T(2,128)S(1)} %bitcast_divide_fusion.4), channel_id=1, source_target_pairs={{0,4},{4,8},{8,12},{12,16},{16,20},{20,24},{24,28},{1,5},{5,9},{9,... | collective-permute-start | bytes 6152 | tf_op jit(solution)/shard_map/while/body/eval_jaxpr/ppermute | solution.py:13
  176.7 6.4 %collective-permute-start.1 = (f32[2,256]{1,0:T(2,128)S(1)}, f32[2,256]{1,0:T(2,128)S(1)}, u32[]{:S(2)}, u32[]{:S(2)}) collective-permute-start(f32[2,256]{1,0:T(2,128)S(1)} %bitcast_divide_fusion.5), channel_id=1, source_target_pairs={{4,0},{8,4},{12,8},{16,12},{20,16},{24,20},{28,24},{5,1},{9,5},{13... | collective-permute-start | bytes 6152 | tf_op jit(solution)/shard_map/while/body/eval_jaxpr/ppermute | solution.py:13
  179.2 6.4 %collective-permute-start = (f32[2,256]{1,0:T(2,128)S(1)}, f32[2,256]{1,0:T(2,128)S(1)}, u32[]{:S(2)}, u32[]{:S(2)}) collective-permute-start(f32[2,256]{1,0:T(2,128)S(1)} %bitcast_divide_fusion.4), channel_id=1, source_target_pairs={{0,4},{4,8},{8,12},{12,16},{16,20},{20,24},{24,28},{1,5},{5,9},{9,... | collective-permute-start | bytes 6152 | tf_op jit(solution)/shard_map/while/body/eval_jaxpr/ppermute | solution.py:13
  186.3 6.4 %collective-permute-start.1 = (f32[2,256]{1,0:T(2,128)S(1)}, f32[2,256]{1,0:T(2,128)S(1)}, u32[]{:S(2)}, u32[]{:S(2)}) collective-permute-start(f32[2,256]{1,0:T(2,128)S(1)} %bitcast_divide_fusion.5), channel_id=1, source_target_pairs={{4,0},{8,4},{12,8},{16,12},{20,16},{24,20},{28,24},{5,1},{9,5},{13... | collective-permute-start | bytes 6152 | tf_op jit(solution)/shard_map/while/body/eval_jaxpr/ppermute | solution.py:13
  188.8 6.4 %collective-permute-start = (f32[2,256]{1,0:T(2,128)S(1)}, f32[2,256]{1,0:T(2,128)S(1)}, u32[]{:S(2)}, u32[]{:S(2)}) collective-permute-start(f32[2,256]{1,0:T(2,128)S(1)} %bitcast_divide_fusion.4), channel_id=1, source_target_pairs={{0,4},{4,8},{8,12},{12,16},{16,20},{20,24},{24,28},{1,5},{5,9},{9,... | collective-permute-start | bytes 6152 | tf_op jit(solution)/shard_map/while/body/eval_jaxpr/ppermute | solution.py:13
  195.9 6.4 %collective-permute-start.1 = (f32[2,256]{1,0:T(2,128)S(1)}, f32[2,256]{1,0:T(2,128)S(1)}, u32[]{:S(2)}, u32[]{:S(2)}) collective-permute-start(f32[2,256]{1,0:T(2,128)S(1)} %bitcast_divide_fusion.5), channel_id=1, source_target_pairs={{4,0},{8,4},{12,8},{16,12},{20,16},{24,20},{28,24},{5,1},{9,5},{13... | collective-permute-start | bytes 6152 | tf_op jit(solution)/shard_map/while/body/eval_jaxpr/ppermute | solution.py:13
  198.4 6.4 %collective-permute-start = (f32[2,256]{1,0:T(2,128)S(1)}, f32[2,256]{1,0:T(2,128)S(1)}, u32[]{:S(2)}, u32[]{:S(2)}) collective-permute-start(f32[2,256]{1,0:T(2,128)S(1)} %bitcast_divide_fusion.4), channel_id=1, source_target_pairs={{0,4},{4,8},{8,12},{12,16},{16,20},{20,24},{24,28},{1,5},{5,9},{9,... | collective-permute-start | bytes 6152 | tf_op jit(solution)/shard_map/while/body/eval_jaxpr/ppermute | solution.py:13
  205.5 6.4 %collective-permute-start.1 = (f32[2,256]{1,0:T(2,128)S(1)}, f32[2,256]{1,0:T(2,128)S(1)}, u32[]{:S(2)}, u32[]{:S(2)}) collective-permute-start(f32[2,256]{1,0:T(2,128)S(1)} %bitcast_divide_fusion.5), channel_id=1, source_target_pairs={{4,0},{8,4},{12,8},{16,12},{20,16},{24,20},{28,24},{5,1},{9,5},{13... | collective-permute-start | bytes 6152 | tf_op jit(solution)/shard_map/while/body/eval_jaxpr/ppermute | solution.py:13
  208.0 6.4 %collective-permute-start = (f32[2,256]{1,0:T(2,128)S(1)}, f32[2,256]{1,0:T(2,128)S(1)}, u32[]{:S(2)}, u32[]{:S(2)}) collective-permute-start(f32[2,256]{1,0:T(2,128)S(1)} %bitcast_divide_fusion.4), channel_id=1, source_target_pairs={{0,4},{4,8},{8,12},{12,16},{16,20},{20,24},{24,28},{1,5},{5,9},{9,... | collective-permute-start | bytes 6152 | tf_op jit(solution)/shard_map/while/body/eval_jaxpr/ppermute | solution.py:13
  215.2 6.4 %collective-permute-start.1 = (f32[2,256]{1,0:T(2,128)S(1)}, f32[2,256]{1,0:T(2,128)S(1)}, u32[]{:S(2)}, u32[]{:S(2)}) collective-permute-start(f32[2,256]{1,0:T(2,128)S(1)} %bitcast_divide_fusion.5), channel_id=1, source_target_pairs={{4,0},{8,4},{12,8},{16,12},{20,16},{24,20},{28,24},{5,1},{9,5},{13... | collective-permute-start | bytes 6152 | tf_op jit(solution)/shard_map/while/body/eval_jaxpr/ppermute | solution.py:13
  217.6 6.4 %collective-permute-start = (f32[2,256]{1,0:T(2,128)S(1)}, f32[2,256]{1,0:T(2,128)S(1)}, u32[]{:S(2)}, u32[]{:S(2)}) collective-permute-start(f32[2,256]{1,0:T(2,128)S(1)} %bitcast_divide_fusion.4), channel_id=1, source_target_pairs={{0,4},{4,8},{8,12},{12,16},{16,20},{20,24},{24,28},{1,5},{5,9},{9,... | collective-permute-start | bytes 6152 | tf_op jit(solution)/shard_map/while/body/eval_jaxpr/ppermute | solution.py:13
  224.8 6.4 %collective-permute-start.1 = (f32[2,256]{1,0:T(2,128)S(1)}, f32[2,256]{1,0:T(2,128)S(1)}, u32[]{:S(2)}, u32[]{:S(2)}) collective-permute-start(f32[2,256]{1,0:T(2,128)S(1)} %bitcast_divide_fusion.5), channel_id=1, source_target_pairs={{4,0},{8,4},{12,8},{16,12},{20,16},{24,20},{28,24},{5,1},{9,5},{13... | collective-permute-start | bytes 6152 | tf_op jit(solution)/shard_map/while/body/eval_jaxpr/ppermute | solution.py:13
  227.3 6.4 %collective-permute-start = (f32[2,256]{1,0:T(2,128)S(1)}, f32[2,256]{1,0:T(2,128)S(1)}, u32[]{:S(2)}, u32[]{:S(2)}) collective-permute-start(f32[2,256]{1,0:T(2,128)S(1)} %bitcast_divide_fusion.4), channel_id=1, source_target_pairs={{0,4},{4,8},{8,12},{12,16},{16,20},{20,24},{24,28},{1,5},{5,9},{9,... | collective-permute-start | bytes 6152 | tf_op jit(solution)/shard_map/while/body/eval_jaxpr/ppermute | solution.py:13
  309.3 24.0 %copy-start.1 = (s32[2]{0:T(128)S(1)}, s32[2]{0:T(128)}, u32[]{:S(2)}) copy-start(s32[2]{0:T(128)} %param.14) | copy-start | bytes 28
Sparse Core Ops, SparseCore 0:
  9.5 34.6 all-gather.1
  312.8 121.4 reduce-scatter.1
where the time goes:
time: 510 us; the launch traced here: 507 us
  matrix products  159 us (31%)
  waiting for transfers between devices  150 us (29%)
  blocking collectives  83.6 us (16%)
  starting transfers between devices  41 us (8%)
  other arithmetic  36.2 us (7%)
  local copies, waits for them, and re-layouts  14.3 us (3%)
  between operations  14.2 us (3%)
  loops' own time  8.47 us (2%)
    dot_general x64, matrix products, product_step(): jnp.einsum('nij,jk->nik', carried, transition, precision=highest)  104 us
    reduce_scatter x1, waiting for transfers between devices, shards(): lax.psum_scatter(jax.ops.segment_sum(jnp.where(inside[:, None], occ_rows,...  99.9 us
    psum x1, blocking collectives, shards(): totals = lax.psum(jnp.sum(counts, axis=0), ('tm', 'emit'))  63.1 us
    ppermute x14, starting transfers between devices, from_behind(): return lax.ppermute(value, axis, pairs)  40.9 us
    all_gather x1, waiting for transfers between devices, shards(): block_rows = lax.all_gather(emission, 'emit', axis=0, tiled=True)  31.2 us
    dot_general x64, matrix products, backward_step(): moved = jnp.dot(later_msg * weight_now, transition.T, precision=highest)  27.4 us
    dot_general x64, matrix products, forward_step(): moved = jnp.dot(previous, transition, precision=highest) * weight_now  21.3 us
    psum x1, blocking collectives, shards(): loglik_sum = lax.psum(loglik_local, 'tm')  20.5 us
  transfers between devices with their start and end apart: 16, of which 9 were waited for; matrix products, arithmetic and copies ran while one was open for 2% of the time, Pallas kernels for 0%

commit v1 on v0

--- a/solution.py
+++ b/solution.py
@@ -5,6 +5,18 @@
 
 highest = lax.Precision.HIGHEST
 pseudo_count = 0.01
+
+
+def collect(array, axis, dim):
+    ways, here, hop = (lax.axis_size(axis), lax.axis_index(axis), array.shape[dim])
+    lengths = [n * ways if d == dim else n for d, n in enumerate(array.shape)]
+    full = lax.dynamic_update_slice_in_dim(
+        jnp.zeros(lengths, array.dtype), array, here * hop, axis=dim
+    )
+    for far in range(1, ways):
+        array = lax.ppermute(array, axis, [(d, (d + 1) % ways) for d in range(ways)])
+        full = lax.dynamic_update_slice_in_dim(full, array, (here - far) % ways * hop, axis=dim)
+    return full
 
 
 def from_behind(value, axis, by):
@@ -31,7 +43,7 @@
     total_rows = own_rows * emit_count
     positions = tm_place * frame_count + jnp.arange(frame_count, dtype=jnp.int32)
     active = positions[None, :] >= starts[:, None]
-    block_rows = lax.all_gather(emission, "emit", axis=0, tiled=True)
+    block_rows = collect(emission, "emit", 0)
     local_ids = observed
     inside = (local_ids >= 0) & (local_ids < block_rows.shape[0])
     taken = jnp.take(block_rows, jnp.clip(local_ids, 0, block_rows.shape[0] - 1), axis=0)

time: 510 us -> 453 us (0.89)
  matrix products: 159 us -> 97.8 us
  local copies, waits for them, and re-layouts: 14.3 us -> 20.6 us
    dot_general x64, matrix products: 104 us -> 43.1 us  [product_step(): jnp.einsum('nij,jk->nik', carried, transition, precision=highest)]
    ppermute x0 -> x3, waiting for transfers between devices: none -> 33.1 us  [collect(): lax.ppermute(array, axis, [(d, (d + 1) % ways) for d in range(ways)])]
    all_gather x1 -> x0, waiting for transfers between devices: 31.2 us -> none  [shards(): block_rows = lax.all_gather(emission, 'emit', axis=0, tiled=True)]
    dynamic_update_slice x0 -> x4, local copies, waits for them, and re-layouts: none -> 5.49 us  [the longest x3 4.44 us: collect(): lax.dynamic_update_slice_in_dim(full, array, (here - far) % ways * hop, a...]
  transfers between devices with their start and end apart: 16 -> 18, of which waited for: 9 -> 11; matrix products, arithmetic and copies ran while one was open for 2% -> 3% of each run, Pallas kernels for 0% -> 0%
where the time goes in v1:
time: 453 us; the launch traced here: 452 us
  waiting for transfers between devices  152 us (34%)
  matrix products  97.8 us (22%)
  blocking collectives  83.6 us (18%)
  starting transfers between devices  41 us (9%)
  other arithmetic  35.7 us (8%)
  local copies, waits for them, and re-layouts  20.6 us (5%)
  between operations  14.2 us (3%)
  loops' own time  7.32 us (2%)
    reduce_scatter x1, waiting for transfers between devices, shards(): lax.psum_scatter(jax.ops.segment_sum(jnp.where(inside[:, None], occ_rows,...  100 us
    psum x1, blocking collectives, shards(): totals = lax.psum(jnp.sum(counts, axis=0), ('tm', 'emit'))  63.2 us
    dot_general x64, matrix products, product_step(): jnp.einsum('nij,jk->nik', carried, transition, precision=highest)  43.1 us
    ppermute x14, starting transfers between devices, from_behind(): return lax.ppermute(value, axis, pairs)  40.9 us
    ppermute x3, waiting for transfers between devices, collect(): lax.ppermute(array, axis, [(d, (d + 1) % ways) for d in range(ways)])  33.1 us
    dot_general x64, matrix products, backward_step(): moved = jnp.dot(later_msg * weight_now, transition.T, precision=highest)  27.2 us
    dot_general x64, matrix products, forward_step(): moved = jnp.dot(previous, transition, precision=highest) * weight_now  21.2 us
    psum x1, blocking collectives, shards(): loglik_sum = lax.psum(loglik_local, 'tm')  20.5 us
  transfers between devices with their start and end apart: 18, of which 11 were waited for; matrix products, arithmetic and copies ran while one was open for 3% of the time, Pallas kernels for 0%

profile of v1, /device:TPU:10, one launch (start us, length us, event | category | flops | bytes accessed | tf_op | source)
XLA Modules:
  0.0 451.9 jit_solution(13030395742426601448)
XLA Ops:
  7.3 14.4 %collective-permute-done.2 = f32[1024,256]{1,0:T(8,128)S(1)} collective-permute-done((f32[1024,256]{1,0:T(8,128)}, f32[1024,256]{1,0:T(8,128)S(1)}, u32[]{:S(2)}, u32[]{:S(2)}) %collective-permute-start.2) | collective-permute-done | bytes 1048608 | tf_op jit(solution)/shard_map/ppermute | solution.py:17
  23.3 12.6 %collective-permute-done.3 = f32[1024,256]{1,0:T(8,128)S(1)} collective-permute-done((f32[1024,256]{1,0:T(8,128)S(1)}, f32[1024,256]{1,0:T(8,128)S(1)}, u32[]{:S(2)}, u32[]{:S(2)}) %collective-permute-start.3) | collective-permute-done | bytes 1048608 | tf_op jit(solution)/shard_map/ppermute | solution.py:17
  44.2 6.1 %collective-permute-done.4 = f32[1024,256]{1,0:T(8,128)} collective-permute-done((f32[1024,256]{1,0:T(8,128)S(1)}, f32[1024,256]{1,0:T(8,128)}, u32[]{:S(2)}, u32[]{:S(2)}) %collective-permute-start.4) | collective-permute-done | bytes 1048608 | tf_op jit(solution)/shard_map/ppermute | solution.py:17
  52.5 2.9 gather_fusion
  55.8 56.0 %while.55 = (s32[]{:T(128)}, f32[2,256,256]{2,1,0:T(8,128)S(1)}, pred[64,2]{1,0:T(8,128)(4,1)S(1)}, f32[256,256]{1,0:T(8,128)S(1)}, f32[64,2,256]{2,1,0:T(2,128)S(1)}, /*index=5*/s32[]{:T(128)}) while((s32[]{:T(128)}, f32[2,256,256]{2,1,0:T(8,128)S(1)}, pred[64,2]{1,0:T(8,128)(4,1)S(1)}, f32[256,256]{1,0:T(8,128)S(1)}, ...), condition=%wide.region_3.4_spmd, body=%wide.region_1.3_spmd.sunk | while | flops 403177472 | bytes 2889827 | solution.py:64
  111.8 68.7 %while.58 = (s32[]{:T(128)}, f32[2,256]{1,0:T(2,128)S(1)}, f32[2,256]{1,0:T(2,128)S(1)}, pred[]{:T(512)}, f32[2,256,256]{2,1,0:T(8,128)S(1)}, /*index=5*/pred[]{:T(512)}, f32[256]{0:T(256)S(1)}, s32[]{:T(128)}, s32[]{:T(128)}) while((s32[]{:T(128)}, f32[2,256]{1,0:T(2,128)S(1)}, f32[2,256]{1,0:T(2,128)S(1)}, pred[]{:T(512)}, ...), condition=%wide.region_7.8_spmd.clone, body=%wide.region_4.7_spmd.clone.sunk | while | flops 3149311 | bytes 1098969 | solution.py:82
  112.6 3.3 collective-permute-start.1
  116.5 2.5 collective-permute-start
  119.0 3.8 collective-permute-done
  126.1 3.9 collective-permute-start
  130.1 2.4 collective-permute-done
  135.7 3.9 collective-permute-start
  139.7 2.4 collective-permute-done
  145.3 3.9 collective-permute-start
  149.3 2.4 collective-permute-done
  155.0 3.9 collective-permute-start
  164.6 3.9 collective-permute-start
  174.2 3.9 collective-permute-start
  180.6 37.9 %while.57 = (s32[]{:T(128)}, f32[2,256]{1,0:T(2,128)S(1)}, f32[64,2,256]{2,0,1:T(8,128)S(1)}, pred[64,2]{1,0:T(8,128)(4,1)S(1)}, f32[64,2,256]{2,1,0:T(2,128)S(1...) while((s32[]{:T(128)}, f32[2,256]{1,0:T(2,128)S(1)}, f32[64,2,256]{2,0,1:T(8,128)S(1)}, ...), condition=%wide.region_13.14_spmd, body=%wide.region_11.13_spmd.sunk | while | flops 1574913 | bytes 282763 | solution.py:101
  218.5 35.2 %while.56 = (s32[]{:T(128)}, f32[2,256]{1,0:T(2,128)S(1)}, f32[64,2,256]{2,0,1:T(8,128)S(1)}, f32[64,2]{1,0:T(8,128)S(1)}, pred[64,2]{1,0:T(8,128)(4,1)S(1)}, /*...) while((s32[]{:T(128)}, f32[2,256]{1,0:T(2,128)S(1)}, ...), condition=%wide.region_10.11_spmd, body=%wide.region_8.10_spmd.sunk | while | flops 1574914 | bytes 282793 | solution.py:93
  254.2 3.4 scatter_custom_fusion
  257.6 20.5 %psum.15 = f32[2]{0:T(128)S(1)} all-reduce(f32[2]{0:T(128)S(1)} %reduce_sum.94), channel_id=1, replica_groups=mesh['tm'=8,'emit'=4] {'tm'}, use_global_device_ids=true, to_apply=%region_20.21 | all-reduce | flops 2 | bytes 16 | tf_op jit(solution)/shard_map/psum | solution.py:122
  279.3 100.1 %reduce-scatter.2.cloned.1.call-done = f32[128,256]{1,0:T(8,128)} async-done(((f32[4096,256]{1,0:T(8,128)}), f32[128,256]{1,0:T(8,128)}) %reduce-scatter.2.cloned.1.call-update) | async-done | bytes 131088 | tf_op jit(solution)/shard_map/reduce_scatter | solution.py:111
  380.3 63.2 %psum.14 = f32[256]{0:T(256)S(1)} all-reduce(f32[256]{0:T(256)S(1)} %reduce_sum.93), channel_id=1, replica_groups=mesh['tm'=8,'emit'=4] {'tm','emit'}, use_global_device_ids=true, to_apply=%region_18.19 | all-reduce | flops 256 | bytes 2048 | tf_op jit(solution)/shard_map/psum | solution.py:121
  (1149 shorter events, 166.7 us)
Async XLA Ops:
  7.2 33.1 %copy-start.1 = (f32[1024,256]{1,0:T(8,128)S(1)}, f32[1024,256]{1,0:T(8,128)}, u32[]{:S(2)}) copy-start(f32[1024,256]{1,0:T(8,128)} %param.17) | copy-start | bytes 3145732
  7.2 34.2 %copy-start.2 = (f32[256]{0:T(256)S(1)}, f32[256]{0:T(256)}, u32[]{:S(2)}) copy-start(f32[256]{0:T(256)} %param.15) | copy-start | bytes 3076
  7.2 372.2 %reduce-scatter.2.cloned.1.call-start = ((), (), s32[]{:S(2)}) async-start(), calls=%async_computation.1 | async-start | bytes 4325376 | tf_op jit(solution)/shard_map/reduce_scatter | solution.py:111
  7.2 14.5 %collective-permute-start.2 = (f32[1024,256]{1,0:T(8,128)}, f32[1024,256]{1,0:T(8,128)S(1)}, u32[]{:S(2)}, u32[]{:S(2)}) collective-permute-start(f32[1024,256]{1,0:T(8,128)} %param.17), channel_id=1, source_target_pairs={{0,1},{1,2},{2,3},{3,0},{4,5},{5,6},{6,7},{7,4},{8,9},{9,10},{10,1... | collective-permute-start | bytes 3145736 | tf_op jit(solution)/shard_map/ppermute | solution.py:17
  21.7 14.2 %collective-permute-start.3 = (f32[1024,256]{1,0:T(8,128)S(1)}, f32[1024,256]{1,0:T(8,128)S(1)}, u32[]{:S(2)}, u32[]{:S(2)}) collective-permute-start(f32[1024,256]{1,0:T(8,128)S(1)} %collective-permute-done.2), channel_id=1, source_target_pairs={{0,1},{1,2},{2,3},{3,0},{4,5},{5,6},{6,7},{7,4},{8,9},{9,10},{10,1... | collective-permute-start | bytes 3145736 | tf_op jit(solution)/shard_map/ppermute | solution.py:17
  35.9 14.3 %collective-permute-start.4 = (f32[1024,256]{1,0:T(8,128)S(1)}, f32[1024,256]{1,0:T(8,128)}, u32[]{:S(2)}, u32[]{:S(2)}) collective-permute-start(f32[1024,256]{1,0:T(8,128)S(1)} %collective-permute-done.3), channel_id=1, source_target_pairs={{0,1},{1,2},{2,3},{3,0},{4,5},{5,6},{6,7},{7,4},{8,9},{9,10},{10,1... | collective-permute-start | bytes 3145736 | tf_op jit(solution)/shard_map/ppermute | solution.py:17
  42.0 13.7 %copy-start = (f32[256,256]{1,0:T(8,128)S(1)}, f32[256,256]{1,0:T(8,128)}, u32[]{:S(2)}) copy-start(f32[256,256]{1,0:T(8,128)} %param.16) | copy-start | bytes 786436
  112.6 6.4 %collective-permute-start.1 = (f32[2,256]{1,0:T(2,128)S(1)}, f32[2,256]{1,0:T(2,128)S(1)}, u32[]{:S(2)}, u32[]{:S(2)}) collective-permute-start(f32[2,256]{1,0:T(2,128)S(1)} %bitcast_divide_fusion.5), channel_id=1, source_target_pairs={{4,0},{8,4},{12,8},{16,12},{20,16},{24,20},{28,24},{5,1},{9,5},{13... | collective-permute-start | bytes 6152 | tf_op jit(solution)/shard_map/while/body/eval_jaxpr/ppermute | solution.py:25
  116.5 6.4 %collective-permute-start = (f32[2,256]{1,0:T(2,128)S(1)}, f32[2,256]{1,0:T(2,128)S(1)}, u32[]{:S(2)}, u32[]{:S(2)}) collective-permute-start(f32[2,256]{1,0:T(2,128)S(1)} %bitcast_divide_fusion.4), channel_id=1, source_target_pairs={{0,4},{4,8},{8,12},{12,16},{16,20},{20,24},{24,28},{1,5},{5,9},{9,... | collective-permute-start | bytes 6152 | tf_op jit(solution)/shard_map/while/body/eval_jaxpr/ppermute | solution.py:25
  123.6 6.4 %collective-permute-start.1 = (f32[2,256]{1,0:T(2,128)S(1)}, f32[2,256]{1,0:T(2,128)S(1)}, u32[]{:S(2)}, u32[]{:S(2)}) collective-permute-start(f32[2,256]{1,0:T(2,128)S(1)} %bitcast_divide_fusion.5), channel_id=1, source_target_pairs={{4,0},{8,4},{12,8},{16,12},{20,16},{24,20},{28,24},{5,1},{9,5},{13... | collective-permute-start | bytes 6152 | tf_op jit(solution)/shard_map/while/body/eval_jaxpr/ppermute | solution.py:25
  126.1 6.4 %collective-permute-start = (f32[2,256]{1,0:T(2,128)S(1)}, f32[2,256]{1,0:T(2,128)S(1)}, u32[]{:S(2)}, u32[]{:S(2)}) collective-permute-start(f32[2,256]{1,0:T(2,128)S(1)} %bitcast_divide_fusion.4), channel_id=1, source_target_pairs={{0,4},{4,8},{8,12},{12,16},{16,20},{20,24},{24,28},{1,5},{5,9},{9,... | collective-permute-start | bytes 6152 | tf_op jit(solution)/shard_map/while/body/eval_jaxpr/ppermute | solution.py:25
  133.2 6.4 %collective-permute-start.1 = (f32[2,256]{1,0:T(2,128)S(1)}, f32[2,256]{1,0:T(2,128)S(1)}, u32[]{:S(2)}, u32[]{:S(2)}) collective-permute-start(f32[2,256]{1,0:T(2,128)S(1)} %bitcast_divide_fusion.5), channel_id=1, source_target_pairs={{4,0},{8,4},{12,8},{16,12},{20,16},{24,20},{28,24},{5,1},{9,5},{13... | collective-permute-start | bytes 6152 | tf_op jit(solution)/shard_map/while/body/eval_jaxpr/ppermute | solution.py:25
  135.7 6.4 %collective-permute-start = (f32[2,256]{1,0:T(2,128)S(1)}, f32[2,256]{1,0:T(2,128)S(1)}, u32[]{:S(2)}, u32[]{:S(2)}) collective-permute-start(f32[2,256]{1,0:T(2,128)S(1)} %bitcast_divide_fusion.4), channel_id=1, source_target_pairs={{0,4},{4,8},{8,12},{12,16},{16,20},{20,24},{24,28},{1,5},{5,9},{9,... | collective-permute-start | bytes 6152 | tf_op jit(solution)/shard_map/while/body/eval_jaxpr/ppermute | solution.py:25
  142.8 6.4 %collective-permute-start.1 = (f32[2,256]{1,0:T(2,128)S(1)}, f32[2,256]{1,0:T(2,128)S(1)}, u32[]{:S(2)}, u32[]{:S(2)}) collective-permute-start(f32[2,256]{1,0:T(2,128)S(1)} %bitcast_divide_fusion.5), channel_id=1, source_target_pairs={{4,0},{8,4},{12,8},{16,12},{20,16},{24,20},{28,24},{5,1},{9,5},{13... | collective-permute-start | bytes 6152 | tf_op jit(solution)/shard_map/while/body/eval_jaxpr/ppermute | solution.py:25
  145.3 6.4 %collective-permute-start = (f32[2,256]{1,0:T(2,128)S(1)}, f32[2,256]{1,0:T(2,128)S(1)}, u32[]{:S(2)}, u32[]{:S(2)}) collective-permute-start(f32[2,256]{1,0:T(2,128)S(1)} %bitcast_divide_fusion.4), channel_id=1, source_target_pairs={{0,4},{4,8},{8,12},{12,16},{16,20},{20,24},{24,28},{1,5},{5,9},{9,... | collective-permute-start | bytes 6152 | tf_op jit(solution)/shard_map/while/body/eval_jaxpr/ppermute | solution.py:25
  152.5 6.4 %collective-permute-start.1 = (f32[2,256]{1,0:T(2,128)S(1)}, f32[2,256]{1,0:T(2,128)S(1)}, u32[]{:S(2)}, u32[]{:S(2)}) collective-permute-start(f32[2,256]{1,0:T(2,128)S(1)} %bitcast_divide_fusion.5), channel_id=1, source_target_pairs={{4,0},{8,4},{12,8},{16,12},{20,16},{24,20},{28,24},{5,1},{9,5},{13... | collective-permute-start | bytes 6152 | tf_op jit(solution)/shard_map/while/body/eval_jaxpr/ppermute | solution.py:25
  155.0 6.4 %collective-permute-start = (f32[2,256]{1,0:T(2,128)S(1)}, f32[2,256]{1,0:T(2,128)S(1)}, u32[]{:S(2)}, u32[]{:S(2)}) collective-permute-start(f32[2,256]{1,0:T(2,128)S(1)} %bitcast_divide_fusion.4), channel_id=1, source_target_pairs={{0,4},{4,8},{8,12},{12,16},{16,20},{20,24},{24,28},{1,5},{5,9},{9,... | collective-permute-start | bytes 6152 | tf_op jit(solution)/shard_map/while/body/eval_jaxpr/ppermute | solution.py:25
  162.1 6.4 %collective-permute-start.1 = (f32[2,256]{1,0:T(2,128)S(1)}, f32[2,256]{1,0:T(2,128)S(1)}, u32[]{:S(2)}, u32[]{:S(2)}) collective-permute-start(f32[2,256]{1,0:T(2,128)S(1)} %bitcast_divide_fusion.5), channel_id=1, source_target_pairs={{4,0},{8,4},{12,8},{16,12},{20,16},{24,20},{28,24},{5,1},{9,5},{13... | collective-permute-start | bytes 6152 | tf_op jit(solution)/shard_map/while/body/eval_jaxpr/ppermute | solution.py:25
  164.6 6.4 %collective-permute-start = (f32[2,256]{1,0:T(2,128)S(1)}, f32[2,256]{1,0:T(2,128)S(1)}, u32[]{:S(2)}, u32[]{:S(2)}) collective-permute-start(f32[2,256]{1,0:T(2,128)S(1)} %bitcast_divide_fusion.4), channel_id=1, source_target_pairs={{0,4},{4,8},{8,12},{12,16},{16,20},{20,24},{24,28},{1,5},{5,9},{9,... | collective-permute-start | bytes 6152 | tf_op jit(solution)/shard_map/while/body/eval_jaxpr/ppermute | solution.py:25
  171.7 6.4 %collective-permute-start.1 = (f32[2,256]{1,0:T(2,128)S(1)}, f32[2,256]{1,0:T(2,128)S(1)}, u32[]{:S(2)}, u32[]{:S(2)}) collective-permute-start(f32[2,256]{1,0:T(2,128)S(1)} %bitcast_divide_fusion.5), channel_id=1, source_target_pairs={{4,0},{8,4},{12,8},{16,12},{20,16},{24,20},{28,24},{5,1},{9,5},{13... | collective-permute-start | bytes 6152 | tf_op jit(solution)/shard_map/while/body/eval_jaxpr/ppermute | solution.py:25
  174.2 6.4 %collective-permute-start = (f32[2,256]{1,0:T(2,128)S(1)}, f32[2,256]{1,0:T(2,128)S(1)}, u32[]{:S(2)}, u32[]{:S(2)}) collective-permute-start(f32[2,256]{1,0:T(2,128)S(1)} %bitcast_divide_fusion.4), channel_id=1, source_target_pairs={{0,4},{4,8},{8,12},{12,16},{16,20},{20,24},{24,28},{1,5},{5,9},{9,... | collective-permute-start | bytes 6152 | tf_op jit(solution)/shard_map/while/body/eval_jaxpr/ppermute | solution.py:25
  254.2 23.9 %copy-start.3 = (s32[2]{0:T(128)S(1)}, s32[2]{0:T(128)}, u32[]{:S(2)}) copy-start(s32[2]{0:T(128)} %param.14) | copy-start | bytes 28
Sparse Core Ops, SparseCore 0:
  257.7 121.5 reduce-scatter.1
